TPU v7x, 128 devices: a whole 4x4x4 slice. The times are simulated.
128 devices in a mesh: gx: 8 (over z_hi, x), gy: 16 (over z_lo, y, core).
Axes of the slice: x: 4, y: 4, z: 4 (z_hi: 2, z_lo: 2; z = z_hi * 2 + z_lo), core: 2. Of those that a mesh axis runs over, the one named last changes fastest.
Arguments:
- coarse: bfloat16 [12, 128, 512], P(None, ('gx', 'gy')), may hold values from -6 to 6
- weight_one: bfloat16 [3, 3, 12, 64], replicated, may hold values from -0.625 to 0.625
- weight_two: bfloat16 [3, 3, 64, 64], replicated, may hold values from -0.25 to 0.25
- weight_three: bfloat16 [3, 3, 64, 256], replicated, may hold values from -0.25 to 0.25
- weight_four: bfloat16 [3, 3, 64, 256], replicated, may hold values from -0.25 to 0.25
- weight_five: bfloat16 [3, 3, 64, 12], replicated, may hold values from -0.25 to 0.25
- bias_one: float32 [64], replicated, may hold values from -3 to 3
- bias_two: float32 [64], replicated, may hold values from -3 to 3
- bias_three: float32 [256], replicated, may hold values from -3 to 3
- bias_four: float32 [256], replicated, may hold values from -3 to 3
- bias_five: float32 [12], replicated, may hold values from -3 to 3
- cotangent: bfloat16 [12, 512, 2048], P(None, 'gx', 'gy'), may hold values from -6 to 6
Outputs:
- fine: float32 [12, 512, 2048], P(None, 'gx', 'gy')
- grad_w1: float32 [3, 3, 12, 64], replicated
- grad_w2: float32 [3, 3, 64, 64], replicated
- grad_w3: float32 [3, 3, 64, 256], replicated
- grad_w4: float32 [3, 3, 64, 256], replicated
- grad_w5: float32 [3, 3, 64, 12], replicated
- grad_b1: float32 [64], replicated
- grad_b2: float32 [64], replicated
- grad_b3: float32 [256], replicated
- grad_b4: float32 [256], replicated
- grad_b5: float32 [12], replicated
All inputs are finite; a program needn't handle non-finite values.
Results may differ from a plain program's by a relative error of at most 0.013.
Values may be sent and summed in bfloat16 or wider, within the bound.
A program may use at most 128 MiB of HBM per device.

v0:
```python
import jax
import jax.numpy as jnp
from jax import lax
from jax.sharding import PartitionSpec as P


def padded_2(block, sides, width):
    for axis, dim in sides:
        count = lax.axis_size(axis)
        forward = [(i, i + 1) for i in range(count - 1)]
        backward = [(target, source) for source, target in forward]
        low = lax.ppermute(
            lax.slice_in_dim(block, block.shape[dim] - width, None, axis=dim), axis, forward
        )
        high = lax.ppermute(lax.slice_in_dim(block, 0, width, axis=dim), axis, backward)
        block = jnp.concatenate([low, block, high], axis=dim)
    return block


def conv_valid(padded, weight, bias):
    rows = padded.shape[1] - 2
    cols = padded.shape[2] - 2
    total = jnp.zeros((weight.shape[3], rows, cols), jnp.float32) + bias[:, None, None]
    for row_off in range(3):
        for col_off in range(3):
            total = total + jnp.einsum(
                "chw,co->ohw",
                padded[:, row_off : row_off + rows, col_off : col_off + cols],
                weight[row_off, col_off],
                preferred_element_type=jnp.float32,
            )
    return total


def conv_back(padded, weight):
    rows = padded.shape[1] - 2
    cols = padded.shape[2] - 2
    total = jnp.zeros((weight.shape[2], rows, cols), jnp.float32)
    for row_off in range(3):
        for col_off in range(3):
            total = total + jnp.einsum(
                "ohw,co->chw",
                padded[:, 2 - row_off : 2 - row_off + rows, 2 - col_off : 2 - col_off + cols],
                weight[row_off, col_off],
                preferred_element_type=jnp.float32,
            )
    return total


def weight_grad(padded, grad):
    rows = grad.shape[1]
    cols = grad.shape[2]
    pieces = []
    for row_off in range(3):
        for col_off in range(3):
            pieces.append(
                jnp.einsum(
                    "chw,ohw->co",
                    padded[:, row_off : row_off + rows, col_off : col_off + cols],
                    grad,
                    preferred_element_type=jnp.float32,
                )
            )
    stacked = jnp.stack(pieces)
    return stacked.reshape(3, 3, stacked.shape[1], stacked.shape[2])


def squash(value):
    return jnp.tanh(value)


def slopes(act):
    act_f = act.astype(jnp.float32)
    return 1.0 - act_f * act_f


def shuffle(value):
    chans, rows, cols = value.shape
    return (
        value.reshape(chans // 4, 2, 2, rows, cols)
        .transpose(0, 3, 1, 4, 2)
        .reshape(chans // 4, 2 * rows, 2 * cols)
    )


def unshuffle(value):
    chans, rows, cols = value.shape
    return (
        value.reshape(chans, rows // 2, 2, cols // 2, 2)
        .transpose(0, 2, 4, 1, 3)
        .reshape(4 * chans, rows // 2, cols // 2)
    )


def inside(halo, rows, cols, grain):
    row = lax.axis_index("gx") * rows * grain - halo + jnp.arange(rows * grain + 2 * halo)
    col = lax.axis_index("gy") * cols * grain - halo + jnp.arange(cols * grain + 2 * halo)
    row_ok = (row >= 0) & (row < rows * grain * lax.axis_size("gx"))
    col_ok = (col >= 0) & (col < cols * grain * lax.axis_size("gy"))
    return (row_ok[:, None] & col_ok[None, :])[None]


def trim(value, width):
    return value[:, width : value.shape[1] - width, width : value.shape[2] - width]


def local_terms(padded, grad):
    return (weight_grad(padded, grad), jnp.sum(grad.astype(jnp.float32), axis=(1, 2)))


def local(
    coarse,
    weight_one,
    weight_two,
    weight_three,
    weight_four,
    weight_five,
    bias_one,
    bias_two,
    bias_three,
    bias_four,
    bias_five,
    cotangent,
):
    tile = lax.all_to_all(coarse, "gy", split_axis=2, concat_axis=1, tiled=True)
    rows = tile.shape[1]
    cols = tile.shape[2]
    sides = (("gx", 1), ("gy", 2))
    zero = jnp.bfloat16(0)
    pad_zero = padded_2(tile, sides, 6)
    pad_cot = padded_2(cotangent, sides, 11)

    def clip(value, halo, grain):
        return jnp.where(inside(halo, rows, cols, grain), value.astype(jnp.bfloat16), zero)

    act_one = clip(squash(conv_valid(pad_zero, weight_one, bias_one)), 5, 1)
    act_two = clip(squash(conv_valid(act_one, weight_two, bias_two)), 4, 1)
    act_three = clip(shuffle(squash(conv_valid(act_two, weight_three, bias_three))), 6, 2)
    act_four = clip(shuffle(squash(conv_valid(act_three, weight_four, bias_four))), 10, 4)
    pad_four = trim(act_four, 9)
    fine = conv_valid(pad_four, weight_five, bias_five)
    layer_five = local_terms(pad_four, cotangent)
    back_four = unshuffle(clip(conv_back(pad_cot, weight_five) * slopes(act_four), 10, 4))
    layer_four = local_terms(trim(act_three, 5), trim(back_four, 5))
    back_three = unshuffle(
        clip(conv_back(back_four, weight_four) * slopes(trim(act_three, 2)), 4, 2)
    )
    layer_three = local_terms(trim(act_two, 3), trim(back_three, 2))
    back_two = clip(conv_back(back_three, weight_three) * slopes(trim(act_two, 3)), 1, 1)
    layer_two = local_terms(trim(act_one, 4), trim(back_two, 1))
    back_one = (conv_back(back_two, weight_two) * slopes(trim(act_one, 5))).astype(jnp.bfloat16)
    layer_one = local_terms(trim(pad_zero, 5), back_one)
    totals = lax.psum(
        (
            layer_one[0],
            layer_two[0],
            layer_three[0],
            layer_four[0],
            layer_five[0],
            layer_one[1],
            layer_two[1],
            layer_three[1],
            layer_four[1],
            layer_five[1],
        ),
        ("gx", "gy"),
    )
    cells = 16 * rows * lax.axis_size("gx") * cols * lax.axis_size("gy")
    scale = jnp.float32(cells) ** (-0.5)
    return (fine,) + tuple((scale * total for total in totals))


def solution(mesh):
    in_specs = (
        P(None, ("gx", "gy"), None),
        P(),
        P(),
        P(),
        P(),
        P(),
        P(),
        P(),
        P(),
        P(),
        P(),
        P(None, "gx", "gy"),
    )
    out_specs = (P(None, "gx", "gy"), P(), P(), P(), P(), P(), P(), P(), P(), P(), P())
    return jax.shard_map(local, mesh=mesh, in_specs=in_specs, out_specs=out_specs, check_vma=False)
```

profile of v0, /device:TPU:1, one launch (start us, length us, event | category | flops | bytes accessed | tf_op | source)
XLA Modules:
  0.0 527.5 jit_solution(14935861701973462244)
XLA Ops:
  10.9 7.3 %all-to-all-start = ((bf16[16,2,192]{2,1,0:T(2,128)(2,1)}), bf16[16,2,192]{2,1,0:T(2,128)(2,1)S(1)}, u32[]{:S(2)}, u32[]{:S(2)}) async-start(bf16[16,2,192]{2,1,0:T(2,128)(2,1)} %reshape.410), calls=%async_computation | async-start | bytes 32768 | tf_op jit(solution)/shard_map/all_to_all | solution.py:125
  22.9 4.8 collective-permute-start.4
  28.9 2.3 collective-permute-start
  32.6 5.9 %collective-permute-done = bf16[12,6,32]{2,0,1:T(8,128)(2,1)S(1)} collective-permute-done((bf16[12,6,32]{2,0,1:T(8,128)(2,1)S(1)}, bf16[12,6,32]{2,0,1:T(8,128)(2,1)S(1)}, u32[]{:S(2)}, u32[]{:S(2)}) %collective-permute-start) | collective-permute-done | bytes 4640 | tf_op jit(solution)/shard_map/ppermute | solution.py:12
  38.7 4.3 collective-permute-start.2
  43.1 1.9 collective-permute-start.3
  46.9 2.3 collective-permute-done.3
  59.9 4.6 copy.173
  69.9 2.8 fusion.234
  72.7 2.8 fusion.236
  75.5 2.5 fusion.238
  78.0 6.1 %fusion.56 = bf16[256,42,74]{0,2,1:T(8,128)(2,1)} fusion(f32[42,74,256]{2,1,0:T(8,128)S(1)} %fusion.224, f32[42,74,256]{2,1,0:T(8,128)S(1)} %fusion.226, f32[42,74,256]{2,1,0:T(8,128)S(1)} %fusion.228, f32[42,74,256]{2,1,0:T(8,128)S(1)} %fusion.230, f32[42,74,256]{2,1,0:T(8,128)S(1)} %fusion.232, f32[42,74,256]{2,1,0:T(8,128)} %fusion.234, ...), kind=kOutput, calls=%fused_computation.60 | convolution fusion | flops 109799424 | bytes 29064192 | tf_op jit(solution)/shard_map/chw,co->ohw/dot_general | solution.py:26
  84.1 3.0 copy.175
  87.1 9.5 %copy.176 = bf16[64,42,2,74,2]{0,4,3,2,1:T(2,128)(2,1)} copy(bf16[64,42,2,74,2]{3,4,2,0,1:T(2,128)(2,1)S(1)} %bitcast.649) | data formatting | bytes 3182592 | tf_op jit(solution)/shard_map/convert_element_type | solution.py:134
  96.6 5.6 %convert_element_type.78 = bf16[64,84,148]{0,2,1:T(8,128)(2,1)} reshape(bf16[64,42,2,74,2]{0,4,3,2,1:T(2,128)(2,1)} %copy.176) | data formatting | bytes 3182592 | tf_op jit(solution)/shard_map/convert_element_type | solution.py:134
  102.1 5.1 copy.177
  107.2 1.9 broadcast_select_fusion
  109.1 1.8 fusion.22
  121.1 1.7 fusion.50
  131.0 2.7 copy.253
  133.8 2.5 copy.251
  136.3 2.5 copy.249
  138.8 2.5 copy.247
  141.3 2.5 copy.245
  143.8 2.5 copy.243
  146.4 2.5 copy.241
  148.9 2.5 copy.237
  151.4 2.5 copy.239
  153.9 2.7 add_bitcast_fusion
  158.6 1.9 collective-permute-start.6
  160.5 2.4 collective-permute-start.7
  165.9 1.7 pad_maximum_fusion
  167.6 3.0 fusion.244
  170.7 3.1 fusion.246
  173.7 3.1 fusion.248
  176.8 3.0 fusion.250
  179.8 3.0 fusion.252
  182.8 3.0 fusion.254
  185.9 3.1 fusion.256
  189.0 3.0 fusion.258
  192.0 14.3 %fusion.19 = bf16[64,84,148]{1,0,2:T(8,128)(2,1)S(1)} fusion(f32[84,148,64]{0,2,1:T(8,128)} %fusion.244, f32[84,148,64]{0,2,1:T(8,128)} %fusion.246, f32[84,148,64]{0,2,1:T(8,128)} %fusion.248, f32[84,148,64]{0,2,1:T(8,128)} %fusion.250, f32[84,148,64]{0,2,1:T(8,128)} %fusion.252, f32[84,148,64]{0,2,1:T(8,128)} %fusion.254, f32[84,148,64]{0,2,1:T(8,128)} %fusion.258, ...), kind=kOutput, calls=%fused_computation.21 | convolution fusion | flops 31030272 | bytes 30106624 | tf_op jit(solution)/shard_map/ohw,co->chw/dot_general | solution.py:41
  206.3 3.8 copy.190
  210.1 5.7 %reshape.311 = bf16[64,42,2,74,2]{0,4,3,2,1:T(2,128)(2,1)} reshape(bf16[64,84,148]{0,2,1:T(8,128)(2,1)} %copy.190) | data formatting | bytes 3182592 | tf_op jit(solution)/shard_map/reshape | solution.py:89
  215.8 11.8 %copy.191 = bf16[64,2,2,42,74]{4,2,1,0,3:T(2,128)(2,1)S(1)} copy(bf16[64,2,2,42,74]{0,2,4,1,3:T(2,128)(2,1)} %bitcast.648) | data formatting | bytes 3182592 | tf_op jit(solution)/shard_map/transpose | solution.py:90
  227.6 1.7 fusion.147
  233.2 2.0 slice.916
  237.9 2.2 fusion.157
  240.1 2.2 copy.201
  242.4 5.0 copy.202
  247.4 2.2 fusion.117
  249.6 2.1 convolution_add_fusion.26
  258.0 1.7 fusion.156
  262.3 1.7 fusion.146
  264.1 1.7 fusion.145
  265.8 1.7 fusion.144
  267.5 1.7 fusion.143
  269.3 1.7 fusion.142
  271.0 1.7 fusion.141
  272.7 1.9 fusion.140
  274.7 1.7 fusion.139
  276.4 2.0 copy.300
  290.1 77.8 %all-reduce = (f32[3,3,12,64]{3,2,1,0:T(8,128)S(1)}, f32[3,3,64,12]{2,3,1,0:T(8,128)S(1)}, f32[64]{0:T(128)S(1)}, f32[64]{0:T(128)S(1)}, f32[256]{0:T(256)S(1)}, /*index=5*/f32[256]{0:T(256)S(1)}, f32[12]{0:T(128)S(1)}) all-reduce(f32[3,3,12,64]{3,2,1,0:T(8,128)S(1)} %bitcast.656, ...), channel_id=1, replica_groups=mesh['gx'=8,'gy'=16] {'gx','gy'}, use_global_device_ids=true, to_apply=%region_0.1 | all-reduce | flops 14476 | bytes 115808 | tf_op jit(solution)/shard_map/psum | solution.py:153
  370.8 145.5 %all-reduce.4.cloned.1.call-done = (f32[3,3,64,64]{3,2,1,0:T(8,128)}, f32[3,3,64,256]{3,2,1,0:T(8,128)}, f32[3,3,64,256]{3,2,1,0:T(8,128)}) async-done(((f32[3,3,64,64]{3,2,1,0:T(8,128)}, f32[3,3,64,256]{3,2,1,0:T(8,128)}, f32[3,3,64,256]{3,2,1,0:T(8,128)}), (f32[3,3,64,64]{3,2,1,0:T(8,128)}, f32[3,3,64,256]{3,2,1,0:T(8,128)}, f32[3,3,64,256]{3,2,1,0:T(8,128)})) %all-reduce.4.cloned.1.call-update) | async-done | bytes 1327120 | tf_op jit(solution)/shard_map/psum | solution.py:153
  518.0 2.4 broadcast_multiply_fusion
  (257 shorter events, 83.4 us)
Async XLA Ops:
  7.2 37.9 %copy-start.19 = (bf16[12,64,128]{2,1,0:T(8,128)(2,1)S(1)}, bf16[12,64,128]{2,1,0:T(8,128)(2,1)}, u32[]{:S(2)}) copy-start(bf16[12,64,128]{2,1,0:T(8,128)(2,1)} %param.23) | copy-start | bytes 589828
  8.7 40.7 %copy-start.36 = (bf16[3,3,12,64]{3,2,1,0:T(8,128)(2,1)S(1)}, bf16[3,3,12,64]{3,2,1,0:T(8,128)(2,1)}, u32[]{:S(2)}) copy-start(bf16[3,3,12,64]{3,2,1,0:T(8,128)(2,1)} %param.13) | copy-start | bytes 41476
  10.9 17.4 %all-to-all-start = ((bf16[16,2,192]{2,1,0:T(2,128)(2,1)}), bf16[16,2,192]{2,1,0:T(2,128)(2,1)S(1)}, u32[]{:S(2)}, u32[]{:S(2)}) async-start(bf16[16,2,192]{2,1,0:T(2,128)(2,1)} %reshape.410), calls=%async_computation | async-start | bytes 32768 | tf_op jit(solution)/shard_map/all_to_all | solution.py:125
  18.2 498.1 %all-reduce.4.cloned.1.call-start = ((), (), s32[]{:S(2)}) async-start(), calls=%async_computation.1 | async-start | bytes 2949120 | tf_op jit(solution)/shard_map/psum | solution.py:153
  20.4 137.2 %collective-permute-start.5 = (bf16[12,11,128]{1,0,2:T(8,128)(2,1)}, bf16[12,11,128]{1,0,2:T(8,128)(2,1)}, u32[]{:S(2)}, u32[]{:S(2)}) collective-permute-start(bf16[12,11,128]{1,0,2:T(8,128)(2,1)} %copy.188), channel_id=1, source_target_pairs={{16,0},{32,16},{48,32},{64,48},{80,64},{96,80},{112,96},{17,1},{33... | collective-permute-start | bytes 101384 | tf_op jit(solution)/shard_map/ppermute | solution.py:15
  22.9 134.7 %collective-permute-start.4 = (bf16[12,11,128]{1,0,2:T(8,128)(2,1)}, bf16[12,11,128]{1,0,2:T(8,128)(2,1)}, u32[]{:S(2)}, u32[]{:S(2)}) collective-permute-start(bf16[12,11,128]{1,0,2:T(8,128)(2,1)} %copy.187), channel_id=1, source_target_pairs={{0,16},{16,32},{32,48},{48,64},{64,80},{80,96},{96,112},{1,17},{17... | collective-permute-start | bytes 101384 | tf_op jit(solution)/shard_map/ppermute | solution.py:12
  28.9 22.1 %copy-start.31 = (bf16[12,16,32]{2,0,1:T(8,128)(2,1)}, bf16[12,16,32]{2,0,1:T(8,128)(2,1)S(1)}, u32[]{:S(2)}) copy-start(bf16[12,16,32]{2,0,1:T(8,128)(2,1)S(1)} %copy.169) | copy-start | bytes 36868
  28.9 9.6 %collective-permute-start = (bf16[12,6,32]{2,0,1:T(8,128)(2,1)S(1)}, bf16[12,6,32]{2,0,1:T(8,128)(2,1)S(1)}, u32[]{:S(2)}, u32[]{:S(2)}) collective-permute-start(bf16[12,6,32]{2,0,1:T(8,128)(2,1)S(1)} %get-tuple-element.72), channel_id=1, source_target_pairs={{0,16},{16,32},{32,48},{48,64},{64,80},{80,96},{96,112},{1,17},{17... | collective-permute-start | bytes 13832 | tf_op jit(solution)/shard_map/ppermute | solution.py:12
  31.3 7.3 %collective-permute-start.1 = (bf16[12,6,32]{2,0,1:T(8,128)(2,1)S(1)}, bf16[12,6,32]{2,0,1:T(8,128)(2,1)S(1)}, u32[]{:S(2)}, u32[]{:S(2)}) collective-permute-start(bf16[12,6,32]{2,0,1:T(8,128)(2,1)S(1)} %get-tuple-element.71), channel_id=1, source_target_pairs={{16,0},{32,16},{48,32},{64,48},{80,64},{96,80},{112,96},{17,1},{33... | collective-permute-start | bytes 13832 | tf_op jit(solution)/shard_map/ppermute | solution.py:15
  38.6 4.5 copy-start.39
  38.6 4.5 copy-start.37
  38.6 12.8 %copy-start.8 = (bf16[12,28,32]{2,0,1:T(8,128)(2,1)}, bf16[12,28,32]{2,0,1:T(8,128)(2,1)S(1)}, u32[]{:S(2)}) copy-start(bf16[12,28,32]{2,0,1:T(8,128)(2,1)S(1)} %constant_dynamic-update-slice_fusion) | copy-start | bytes 64516
  38.7 8.2 %collective-permute-start.2 = (bf16[12,28,6]{2,0,1:T(8,128)(2,1)S(1)}, bf16[12,28,6]{2,0,1:T(8,128)(2,1)S(1)}, u32[]{:S(2)}, u32[]{:S(2)}) collective-permute-start(bf16[12,28,6]{2,0,1:T(8,128)(2,1)S(1)} %get-tuple-element.69), channel_id=1, source_target_pairs={{0,1},{1,2},{2,3},{3,4},{4,5},{5,6},{6,7},{7,8},{8,9},{9,10},{10,1... | collective-permute-start | bytes 12104 | tf_op jit(solution)/shard_map/ppermute | solution.py:12
  43.1 6.1 %collective-permute-start.3 = (bf16[12,28,6]{2,0,1:T(8,128)(2,1)S(1)}, bf16[12,28,6]{2,0,1:T(8,128)(2,1)S(1)}, u32[]{:S(2)}, u32[]{:S(2)}) collective-permute-start(bf16[12,28,6]{2,0,1:T(8,128)(2,1)S(1)} %get-tuple-element.70), channel_id=1, source_target_pairs={{1,0},{2,1},{3,2},{4,3},{5,4},{6,5},{7,6},{8,7},{9,8},{10,9},{11,1... | collective-permute-start | bytes 12104 | tf_op jit(solution)/shard_map/ppermute | solution.py:15
  46.9 4.7 copy-start.17
  49.2 2.5 copy-start.15
  50.2 2.3 copy-start.44
  52.6 0.9 copy-start.27
  52.6 0.9 copy-start.45
  53.5 2.2 copy-start.6
  54.8 1.1 copy-start.22
  54.8 1.1 copy-start.43
  56.0 2.2 copy-start.3
  64.5 1.0 copy-start.20
  75.5 2.5 copy-start.42
  107.2 1.9 copy-start.33
  121.1 3.4 copy-start.12
  146.3 7.6 %copy-start.46 = (f32[12]{0:T(128)S(1)}, f32[12]{0:T(128)}, u32[]{:S(2)}) copy-start(f32[12]{0:T(128)} %param.22) | copy-start | bytes 148
  153.9 2.7 copy-start.13
  158.6 6.1 %collective-permute-start.6 = (bf16[12,86,11]{1,0,2:T(8,128)(2,1)S(1)}, bf16[12,86,11]{1,0,2:T(8,128)(2,1)S(1)}, u32[]{:S(2)}, u32[]{:S(2)}) collective-permute-start(bf16[12,86,11]{1,0,2:T(8,128)(2,1)S(1)} %get-tuple-element.65), channel_id=1, source_target_pairs={{0,1},{1,2},{2,3},{3,4},{4,5},{5,6},{6,7},{7,8},{8,9},{9,10},{10,1... | collective-permute-start | bytes 68120 | tf_op jit(solution)/shard_map/ppermute | solution.py:12
  160.5 5.4 %collective-permute-start.7 = (bf16[12,86,11]{1,0,2:T(8,128)(2,1)S(1)}, bf16[12,86,11]{1,0,2:T(8,128)(2,1)S(1)}, u32[]{:S(2)}, u32[]{:S(2)}) collective-permute-start(bf16[12,86,11]{1,0,2:T(8,128)(2,1)S(1)} %get-tuple-element.66), channel_id=1, source_target_pairs={{1,0},{2,1},{3,2},{4,3},{5,4},{6,5},{7,6},{8,7},{9,8},{10,9},{11,1... | collective-permute-start | bytes 68120 | tf_op jit(solution)/shard_map/ppermute | solution.py:15
  163.8 6.9 %copy-start.34 = (f32[9,64,12]{1,2,0:T(8,128)}, f32[9,64,12]{1,2,0:T(8,128)S(1)}, u32[]{:S(2)}) copy-start(f32[9,64,12]{1,2,0:T(8,128)S(1)} %fusion.220) | copy-start | bytes 82948
  189.0 3.0 copy-start.2
  227.6 1.7 copy-start.21
  247.4 4.3 copy-start
  247.4 4.3 copy-start.23
  254.2 1.6 copy-start.4
  256.3 1.7 copy-start.10
  276.4 2.3 copy-start.11
  276.4 2.3 copy-start.24
  276.4 2.3 copy-start.28
  278.7 1.4 copy-start.7
  278.9 1.4 copy-start.9
  278.9 1.4 copy-start.18
  279.1 1.5 copy-start.32
  279.1 1.5 copy-start.40
  279.1 1.7 copy-start.16
  279.3 2.3 copy-start.29
  282.0 1.3 copy-start.1
  282.0 1.3 copy-start.5
  282.1 1.5 copy-start.25
  283.6 1.9 copy-start.30
  286.7 1.9 copy-start.14
  287.3 2.3 copy-start.38
  287.9 2.2 copy-start.35
  288.0 2.2 copy-start.41
  288.6 80.4 %copy-start.26 = (f32[9,64,256]{2,1,0:T(8,128)}, f32[9,64,256]{2,1,0:T(8,128)S(1)}, u32[]{:S(2)}) copy-start(f32[9,64,256]{2,1,0:T(8,128)S(1)} %fusion.130) | copy-start | bytes 1769476
Sparse Core Ops, SparseCore 0:
  369.2 147.1 all-reduce.3
where the time goes:
time: 537 us; the launch traced here: 527 us
  waiting for transfers between devices  155 us (29%)
  matrix products  138 us (26%)
  local copies, waits for them, and re-layouts  96.1 us (18%)
  blocking collectives  77.8 us (14%)
  starting transfers between devices  27.7 us (5%)
  other arithmetic  17.7 us (3%)
  between operations  15.4 us (3%)
    psum x1, waiting for transfers between devices, local(): lax.psum((layer_one[0], layer_two[0], layer_three[0], layer_four[0], laye...  145 us
    psum x1, blocking collectives, local(): lax.psum((layer_one[0], layer_two[0], layer_three[0], layer_four[0], laye...  77.8 us
    dot_general x36, matrix products, conv_back(): jnp.einsum('ohw,co->chw', padded[:, 2 - row_off:2 - row_off + rows, 2 - c...  59.3 us
    dot_general x45, matrix products, conv_valid(): jnp.einsum('chw,co->ohw', padded[:, row_off:row_off + rows, col_off:col_o...  42.6 us
    dot_general x45, matrix products, weight_grad(): jnp.einsum('chw,ohw->co', padded[:, row_off:row_off + rows, col_off:col_o...  36 us
    convert_element_type x8, local copies, waits for them, and re-layouts, clip(): value.astype(jnp.bfloat16)  29.8 us
    dot_general x9, local copies, waits for them, and re-layouts, conv_valid(): jnp.einsum('chw,co->ohw', padded[:, row_off:row_off + rows, col_off:col_o...  22.9 us
    transpose x2, local copies, waits for them, and re-layouts, unshuffle(): return value.reshape(chans, rows // 2, 2, cols // 2, 2).transpose(0, 2, 4...  16.8 us
  transfers between devices with their start and end apart: 10, of which 4 were waited for; matrix products, arithmetic and copies ran while one was open for 22% of the time, Pallas kernels for 0%

commit v1 on v0

--- a/solution.py
+++ b/solution.py
@@ -2,6 +2,7 @@
 import jax.numpy as jnp
 from jax import lax
 from jax.sharding import PartitionSpec as P
+from jax.lax import psum
 
 
 def padded_2(block, sides, width):
@@ -150,20 +151,23 @@
     layer_two = local_terms(trim(act_one, 4), trim(back_two, 1))
     back_one = (conv_back(back_two, weight_two) * slopes(trim(act_one, 5))).astype(jnp.bfloat16)
     layer_one = local_terms(trim(pad_zero, 5), back_one)
-    totals = lax.psum(
-        (
-            layer_one[0],
-            layer_two[0],
-            layer_three[0],
-            layer_four[0],
-            layer_five[0],
-            layer_one[1],
-            layer_two[1],
-            layer_three[1],
-            layer_four[1],
-            layer_five[1],
+    totals = psum(
+        psum(
+            (
+                layer_one[0],
+                layer_two[0],
+                layer_three[0],
+                layer_four[0],
+                layer_five[0],
+                layer_one[1],
+                layer_two[1],
+                layer_three[1],
+                layer_four[1],
+                layer_five[1],
+            ),
+            "gx",
         ),
-        ("gx", "gy"),
+        "gy",
     )
     cells = 16 * rows * lax.axis_size("gx") * cols * lax.axis_size("gy")
     scale = jnp.float32(cells) ** (-0.5)

time: 537 us -> 515 us (0.959)
  the two profiles are of different devices: /device:TPU:1 before, /device:TPU:25 now
where the time goes in v1:
time: 515 us; the launch traced here: 506 us
  matrix products  132 us (26%)
  waiting for transfers between devices  121 us (23%)
  blocking collectives  97.4 us (19%)
  local copies, waits for them, and re-layouts  95.7 us (19%)
  starting transfers between devices  26.9 us (5%)
  other arithmetic  17.7 us (3%)
  between operations  15.5 us (3%)
    psum x1, waiting for transfers between devices, local(): psum((layer_one[0], layer_two[0], layer_three[0], layer_four[0], layer_fi...  80.9 us
    psum x1, blocking collectives, local(): psum(psum((layer_one[0], layer_two[0], layer_three[0], layer_four[0], lay...  63.3 us
    dot_general x36, matrix products, conv_back(): jnp.einsum('ohw,co->chw', padded[:, 2 - row_off:2 - row_off + rows, 2 - c...  57.9 us
    dot_general x45, matrix products, conv_valid(): jnp.einsum('chw,co->ohw', padded[:, row_off:row_off + rows, col_off:col_o...  42.6 us
    psum x1, blocking collectives, local(): psum((layer_one[0], layer_two[0], layer_three[0], layer_four[0], layer_fi...  34.1 us
    dot_general x45, matrix products, weight_grad(): jnp.einsum('chw,ohw->co', padded[:, row_off:row_off + rows, col_off:col_o...  31.8 us
    convert_element_type x8, local copies, waits for them, and re-layouts, clip(): value.astype(jnp.bfloat16)  29.8 us
    psum x1, waiting for transfers between devices, local(): psum(psum((layer_one[0], layer_two[0], layer_three[0], layer_four[0], lay...  26.6 us
  transfers between devices with their start and end apart: 11, of which 5 were waited for; matrix products, arithmetic and copies ran while one was open for 25% of the time, Pallas kernels for 0%

profile of v1, /device:TPU:25, one launch (start us, length us, event | category | flops | bytes accessed | tf_op | source)
XLA Modules:
  0.0 506.3 jit_solution(6619405552091767639)
XLA Ops:
  10.9 6.4 %all-to-all-start = ((bf16[16,2,192]{2,1,0:T(2,128)(2,1)}), bf16[16,2,192]{2,1,0:T(2,128)(2,1)S(1)}, u32[]{:S(2)}, u32[]{:S(2)}) async-start(bf16[16,2,192]{2,1,0:T(2,128)(2,1)} %reshape.410), calls=%async_computation | async-start | bytes 32768 | tf_op jit(solution)/shard_map/all_to_all | solution.py:126
  21.9 4.8 collective-permute-start.4
  27.9 2.3 collective-permute-start
  31.6 5.6 %collective-permute-done = bf16[12,6,32]{2,0,1:T(8,128)(2,1)S(1)} collective-permute-done((bf16[12,6,32]{2,0,1:T(8,128)(2,1)S(1)}, bf16[12,6,32]{2,0,1:T(8,128)(2,1)S(1)}, u32[]{:S(2)}, u32[]{:S(2)}) %collective-permute-start) | collective-permute-done | bytes 4640 | tf_op jit(solution)/shard_map/ppermute | solution.py:13
  37.4 4.5 collective-permute-start.2
  41.9 1.9 collective-permute-start.3
  45.8 4.4 collective-permute-done.3
  60.8 4.6 copy.173
  70.8 2.8 fusion.234
  73.6 2.8 fusion.236
  76.4 2.5 fusion.238
  78.9 6.1 %fusion.56 = bf16[256,42,74]{0,2,1:T(8,128)(2,1)} fusion(f32[42,74,256]{2,1,0:T(8,128)S(1)} %fusion.224, f32[42,74,256]{2,1,0:T(8,128)S(1)} %fusion.226, f32[42,74,256]{2,1,0:T(8,128)S(1)} %fusion.228, f32[42,74,256]{2,1,0:T(8,128)S(1)} %fusion.230, f32[42,74,256]{2,1,0:T(8,128)S(1)} %fusion.232, f32[42,74,256]{2,1,0:T(8,128)} %fusion.234, ...), kind=kOutput, calls=%fused_computation.60 | convolution fusion | flops 109799424 | bytes 29064192 | tf_op jit(solution)/shard_map/chw,co->ohw/dot_general | solution.py:27
  85.0 3.0 copy.175
  88.1 9.4 %copy.176 = bf16[64,42,2,74,2]{0,4,3,2,1:T(2,128)(2,1)} copy(bf16[64,42,2,74,2]{3,4,2,0,1:T(2,128)(2,1)S(1)} %bitcast.649) | data formatting | bytes 3182592 | tf_op jit(solution)/shard_map/convert_element_type | solution.py:135
  97.4 5.6 %convert_element_type.78 = bf16[64,84,148]{0,2,1:T(8,128)(2,1)} reshape(bf16[64,42,2,74,2]{0,4,3,2,1:T(2,128)(2,1)} %copy.176) | data formatting | bytes 3182592 | tf_op jit(solution)/shard_map/convert_element_type | solution.py:135
  103.0 5.1 %copy.177 = bf16[64,84,148]{1,0,2:T(8,128)(2,1)} copy(bf16[64,84,148]{0,2,1:T(8,128)(2,1)} %convert_element_type.78) | data formatting | bytes 3182592 | tf_op jit(solution)/shard_map/convert_element_type | solution.py:135
  108.1 1.9 broadcast_select_fusion
  110.0 1.8 fusion.22
  113.5 1.7 fusion.30
  115.2 1.7 fusion.34
  116.9 1.7 fusion.38
  118.6 1.7 fusion.42
  120.3 1.7 fusion.46
  122.0 1.7 fusion.50
  123.8 1.7 fusion.54
  131.9 2.7 copy.253
  134.7 2.5 copy.251
  137.2 2.5 copy.249
  139.7 2.5 copy.247
  142.2 2.5 copy.245
  144.8 2.5 copy.243
  147.3 2.5 copy.241
  149.8 2.5 copy.237
  152.3 2.5 copy.239
  154.8 2.7 add_bitcast_fusion
  159.5 1.9 collective-permute-start.6
  161.4 2.4 collective-permute-start.7
  165.6 3.3 collective-permute-done.7
  168.9 1.7 pad_maximum_fusion
  170.6 3.0 fusion.244
  173.7 3.0 fusion.246
  176.7 3.1 fusion.248
  179.8 3.0 fusion.250
  182.8 3.0 fusion.252
  185.9 3.1 fusion.254
  188.9 3.1 fusion.256
  192.0 3.0 fusion.258
  195.0 14.3 %fusion.19 = bf16[64,84,148]{1,0,2:T(8,128)(2,1)S(1)} fusion(f32[84,148,64]{0,2,1:T(8,128)} %fusion.244, f32[84,148,64]{0,2,1:T(8,128)} %fusion.246, f32[84,148,64]{0,2,1:T(8,128)} %fusion.248, f32[84,148,64]{0,2,1:T(8,128)} %fusion.250, f32[84,148,64]{0,2,1:T(8,128)} %fusion.252, f32[84,148,64]{0,2,1:T(8,128)} %fusion.254, f32[84,148,64]{0,2,1:T(8,128)} %fusion.258, ...), kind=kOutput, calls=%fused_computation.21 | convolution fusion | flops 31030272 | bytes 30106624 | tf_op jit(solution)/shard_map/ohw,co->chw/dot_general | solution.py:42
  209.3 3.9 copy.190
  213.2 5.7 %reshape.311 = bf16[64,42,2,74,2]{0,4,3,2,1:T(2,128)(2,1)} reshape(bf16[64,84,148]{0,2,1:T(8,128)(2,1)} %copy.190) | data formatting | bytes 3182592 | tf_op jit(solution)/shard_map/reshape | solution.py:90
  218.9 11.8 %copy.191 = bf16[64,2,2,42,74]{4,2,1,0,3:T(2,128)(2,1)S(1)} copy(bf16[64,2,2,42,74]{0,2,4,1,3:T(2,128)(2,1)} %bitcast.648) | data formatting | bytes 3182592 | tf_op jit(solution)/shard_map/transpose | solution.py:91
  230.7 1.7 fusion.147
  239.0 2.2 fusion.157
  241.2 2.2 copy.201
  243.5 5.0 copy.202
  248.5 2.2 fusion.117
  250.7 2.1 convolution_add_fusion.26
  277.9 2.0 slice.916
  279.9 2.0 copy.300
  286.5 80.9 %all-reduce.9.cloned.1.call-done = (f32[3,3,64,64]{3,2,1,0:T(8,128)}, f32[3,3,64,256]{3,2,1,0:T(8,128)}, f32[3,3,64,256]{3,2,1,0:T(8,128)}) async-done(((f32[3,3,64,64]{3,2,1,0:T(8,128)}, f32[3,3,64,256]{3,2,1,0:T(8,128)}, f32[3,3,64,256]{3,2,1,0:T(8,128)}), (f32[3,3,64,64]{3,2,1,0:T(8,128)}, f32[3,3,64,256]{3,2,1,0:T(8,128)}, f32[3,3,64,256]{3,2,1,0:T(8,128)})) %all-reduce.9.cloned.1.call-update) | async-done | bytes 1327120 | tf_op jit(solution)/shard_map/psum | solution.py:155
  368.3 34.1 %all-reduce.2 = (f32[3,3,12,64]{3,2,1,0:T(8,128)S(1)}, f32[3,3,64,12]{2,3,1,0:T(8,128)S(1)}, f32[64]{0:T(128)S(1)}, f32[64]{0:T(128)S(1)}, f32[256]{0:T(256)S(1)}, /*index=5*/f32[256]{0:T(256)S(1)}, f32[12]{0:T(128)S(1)}) all-reduce(f32[3,3,12,64]{3,2,1,0:T(8,128)S(1)} %bitcast.657, ...), channel_id=1, replica_groups=mesh['gx'=8,'gy'=16] {'gx'}, use_global_device_ids=true, to_apply=%region_0.1 | all-reduce | flops 14476 | bytes 115808 | tf_op jit(solution)/shard_map/psum | solution.py:155
  402.5 63.3 %all-reduce = (f32[3,3,12,64]{3,2,1,0:T(8,128)S(1)}, f32[3,3,64,12]{2,3,1,0:T(8,128)S(1)}, f32[64]{0:T(128)S(1)}, f32[64]{0:T(128)S(1)}, f32[256]{0:T(256)S(1)}, /*index=5*/f32[256]{0:T(256)S(1)}, f32[12]{0:T(128)S(1)}) all-reduce(f32[3,3,12,64]{3,2,1,0:T(8,128)S(1)} %get-tuple-element.65, ...), channel_id=1, replica_groups=mesh['gx'=8,'gy'=16] {'gy'}, use_global_device_ids=true, to_apply=%region_1.2 | all-reduce | flops 14476 | bytes 115808 | tf_op jit(solution)/shard_map/psum | solution.py:154
  468.6 26.6 %all-reduce.7.cloned.1.call-done = (f32[3,3,64,64]{3,2,1,0:T(8,128)}, f32[3,3,64,256]{3,2,1,0:T(8,128)}, f32[3,3,64,256]{3,2,1,0:T(8,128)}) async-done(((f32[3,3,64,64]{3,2,1,0:T(8,128)}, f32[3,3,64,256]{3,2,1,0:T(8,128)}, f32[3,3,64,256]{3,2,1,0:T(8,128)}), (f32[3,3,64,64]{3,2,1,0:T(8,128)}, f32[3,3,64,256]{3,2,1,0:T(8,128)}, f32[3,3,64,256]{3,2,1,0:T(8,128)})) %all-reduce.7.cloned.1.call-update) | async-done | bytes 1327120 | tf_op jit(solution)/shard_map/psum | solution.py:154
  496.9 2.4 broadcast_multiply_fusion
  (271 shorter events, 81.8 us)
Async XLA Ops:
  7.2 36.7 %copy-start.22 = (bf16[12,64,128]{2,1,0:T(8,128)(2,1)S(1)}, bf16[12,64,128]{2,1,0:T(8,128)(2,1)}, u32[]{:S(2)}) copy-start(bf16[12,64,128]{2,1,0:T(8,128)(2,1)} %param.23) | copy-start | bytes 589828
  8.7 41.7 %copy-start.41 = (bf16[3,3,12,64]{3,2,1,0:T(8,128)(2,1)S(1)}, bf16[3,3,12,64]{3,2,1,0:T(8,128)(2,1)}, u32[]{:S(2)}) copy-start(bf16[3,3,12,64]{3,2,1,0:T(8,128)(2,1)} %param.13) | copy-start | bytes 41476
  10.9 16.4 %all-to-all-start = ((bf16[16,2,192]{2,1,0:T(2,128)(2,1)}), bf16[16,2,192]{2,1,0:T(2,128)(2,1)S(1)}, u32[]{:S(2)}, u32[]{:S(2)}) async-start(bf16[16,2,192]{2,1,0:T(2,128)(2,1)} %reshape.410), calls=%async_computation | async-start | bytes 32768 | tf_op jit(solution)/shard_map/all_to_all | solution.py:126
  17.3 350.1 %all-reduce.9.cloned.1.call-start = ((), (), s32[]{:S(2)}) async-start(), calls=%async_computation.2 | async-start | bytes 2949120 | tf_op jit(solution)/shard_map/psum | solution.py:155
  19.4 139.1 %collective-permute-start.5 = (bf16[12,11,128]{1,0,2:T(8,128)(2,1)}, bf16[12,11,128]{1,0,2:T(8,128)(2,1)}, u32[]{:S(2)}, u32[]{:S(2)}) collective-permute-start(bf16[12,11,128]{1,0,2:T(8,128)(2,1)} %copy.188), channel_id=1, source_target_pairs={{16,0},{32,16},{48,32},{64,48},{80,64},{96,80},{112,96},{17,1},{33... | collective-permute-start | bytes 101384 | tf_op jit(solution)/shard_map/ppermute | solution.py:16
  21.9 136.5 %collective-permute-start.4 = (bf16[12,11,128]{1,0,2:T(8,128)(2,1)}, bf16[12,11,128]{1,0,2:T(8,128)(2,1)}, u32[]{:S(2)}, u32[]{:S(2)}) collective-permute-start(bf16[12,11,128]{1,0,2:T(8,128)(2,1)} %copy.187), channel_id=1, source_target_pairs={{0,16},{16,32},{32,48},{48,64},{64,80},{80,96},{96,112},{1,17},{17... | collective-permute-start | bytes 101384 | tf_op jit(solution)/shard_map/ppermute | solution.py:13
  27.9 24.0 %copy-start.33 = (bf16[12,16,32]{2,0,1:T(8,128)(2,1)}, bf16[12,16,32]{2,0,1:T(8,128)(2,1)S(1)}, u32[]{:S(2)}) copy-start(bf16[12,16,32]{2,0,1:T(8,128)(2,1)S(1)} %copy.169) | copy-start | bytes 36868
  27.9 9.3 %collective-permute-start = (bf16[12,6,32]{2,0,1:T(8,128)(2,1)S(1)}, bf16[12,6,32]{2,0,1:T(8,128)(2,1)S(1)}, u32[]{:S(2)}, u32[]{:S(2)}) collective-permute-start(bf16[12,6,32]{2,0,1:T(8,128)(2,1)S(1)} %get-tuple-element.82), channel_id=1, source_target_pairs={{0,16},{16,32},{32,48},{48,64},{64,80},{80,96},{96,112},{1,17},{17... | collective-permute-start | bytes 13832 | tf_op jit(solution)/shard_map/ppermute | solution.py:13
  30.3 6.9 %collective-permute-start.1 = (bf16[12,6,32]{2,0,1:T(8,128)(2,1)S(1)}, bf16[12,6,32]{2,0,1:T(8,128)(2,1)S(1)}, u32[]{:S(2)}, u32[]{:S(2)}) collective-permute-start(bf16[12,6,32]{2,0,1:T(8,128)(2,1)S(1)} %get-tuple-element.81), channel_id=1, source_target_pairs={{16,0},{32,16},{48,32},{64,48},{80,64},{96,80},{112,96},{17,1},{33... | collective-permute-start | bytes 13832 | tf_op jit(solution)/shard_map/ppermute | solution.py:16
  37.3 4.7 copy-start.44
  37.3 4.6 copy-start.42
  37.3 15.0 %copy-start.7 = (bf16[12,28,32]{2,0,1:T(8,128)(2,1)}, bf16[12,28,32]{2,0,1:T(8,128)(2,1)S(1)}, u32[]{:S(2)}) copy-start(bf16[12,28,32]{2,0,1:T(8,128)(2,1)S(1)} %constant_dynamic-update-slice_fusion) | copy-start | bytes 64516
  37.4 8.3 %collective-permute-start.2 = (bf16[12,28,6]{2,0,1:T(8,128)(2,1)S(1)}, bf16[12,28,6]{2,0,1:T(8,128)(2,1)S(1)}, u32[]{:S(2)}, u32[]{:S(2)}) collective-permute-start(bf16[12,28,6]{2,0,1:T(8,128)(2,1)S(1)} %get-tuple-element.79), channel_id=1, source_target_pairs={{0,1},{1,2},{2,3},{3,4},{4,5},{5,6},{6,7},{7,8},{8,9},{9,10},{10,1... | collective-permute-start | bytes 12104 | tf_op jit(solution)/shard_map/ppermute | solution.py:13
  41.9 8.2 %collective-permute-start.3 = (bf16[12,28,6]{2,0,1:T(8,128)(2,1)S(1)}, bf16[12,28,6]{2,0,1:T(8,128)(2,1)S(1)}, u32[]{:S(2)}, u32[]{:S(2)}) collective-permute-start(bf16[12,28,6]{2,0,1:T(8,128)(2,1)S(1)} %get-tuple-element.80), channel_id=1, source_target_pairs={{1,0},{2,1},{3,2},{4,3},{5,4},{6,5},{7,6},{8,7},{9,8},{10,9},{11,1... | collective-permute-start | bytes 12104 | tf_op jit(solution)/shard_map/ppermute | solution.py:16
  45.8 6.9 %copy-start.19 = (bf16[12,28,6]{2,0,1:T(8,128)(2,1)}, bf16[12,28,6]{2,0,1:T(8,128)(2,1)S(1)}, u32[]{:S(2)}) copy-start(bf16[12,28,6]{2,0,1:T(8,128)(2,1)S(1)} %collective-permute-done.2) | copy-start | bytes 12100
  50.2 2.5 copy-start.16
  51.2 2.3 copy-start.49
  53.5 0.9 copy-start.30
  53.5 0.9 copy-start.50
  54.4 2.2 copy-start.5
  55.8 1.1 copy-start.25
  55.8 1.1 copy-start.48
  56.9 2.3 copy-start.3
  65.4 1.0 copy-start.23
  76.4 2.5 copy-start.47
  108.1 1.9 copy-start.36
  122.0 3.4 copy-start.14
  147.3 7.6 %copy-start.51 = (f32[12]{0:T(128)S(1)}, f32[12]{0:T(128)}, u32[]{:S(2)}) copy-start(f32[12]{0:T(128)} %param.22) | copy-start | bytes 148
  154.8 2.7 copy-start.15
  159.5 6.1 %collective-permute-start.6 = (bf16[12,86,11]{1,0,2:T(8,128)(2,1)S(1)}, bf16[12,86,11]{1,0,2:T(8,128)(2,1)S(1)}, u32[]{:S(2)}, u32[]{:S(2)}) collective-permute-start(bf16[12,86,11]{1,0,2:T(8,128)(2,1)S(1)} %get-tuple-element.75), channel_id=1, source_target_pairs={{0,1},{1,2},{2,3},{3,4},{4,5},{5,6},{6,7},{7,8},{8,9},{9,10},{10,1... | collective-permute-start | bytes 68120 | tf_op jit(solution)/shard_map/ppermute | solution.py:13
  161.4 7.5 %collective-permute-start.7 = (bf16[12,86,11]{1,0,2:T(8,128)(2,1)S(1)}, bf16[12,86,11]{1,0,2:T(8,128)(2,1)S(1)}, u32[]{:S(2)}, u32[]{:S(2)}) collective-permute-start(bf16[12,86,11]{1,0,2:T(8,128)(2,1)S(1)} %get-tuple-element.76), channel_id=1, source_target_pairs={{1,0},{2,1},{3,2},{4,3},{5,4},{6,5},{7,6},{8,7},{9,8},{10,9},{11,1... | collective-permute-start | bytes 68120 | tf_op jit(solution)/shard_map/ppermute | solution.py:16
  164.7 9.0 %copy-start.39 = (f32[9,64,12]{1,2,0:T(8,128)}, f32[9,64,12]{1,2,0:T(8,128)S(1)}, u32[]{:S(2)}) copy-start(f32[9,64,12]{1,2,0:T(8,128)S(1)} %fusion.220) | copy-start | bytes 82948
  192.0 3.0 copy-start.2
  230.7 1.7 copy-start.24
  248.5 4.3 copy-start
  248.5 4.3 copy-start.26
  255.3 1.6 copy-start.4
  256.1 1.3 copy-start.31
  256.1 1.5 copy-start.6
  256.9 1.5 copy-start.28
  257.4 13.2 %copy-start.10 = (bf16[64,18,34]{0,2,1:T(8,128)(2,1)}, bf16[64,18,34]{0,2,1:T(8,128)(2,1)S(1)}, u32[]{:S(2)}) copy-start(bf16[64,18,34]{0,2,1:T(8,128)(2,1)S(1)} %fusion.127) | copy-start | bytes 235012
  267.5 1.5 copy-start.29
  269.1 8.5 %copy-start.12 = (bf16[64,16,32]{0,2,1:T(8,128)(2,1)}, bf16[64,16,32]{0,2,1:T(8,128)(2,1)S(1)}, u32[]{:S(2)}) copy-start(bf16[64,16,32]{0,2,1:T(8,128)(2,1)S(1)} %get-tuple-element.84) | copy-start | bytes 196612
  270.8 1.9 copy-start.32
  274.6 2.2 copy-start.8
  274.6 2.2 copy-start.20
  274.6 2.5 copy-start.34
  274.6 2.5 copy-start.45
  274.6 2.7 copy-start.17
  275.9 0.8 copy-start.27
  276.7 218.5 %all-reduce.7.cloned.1.call-start = ((), (), s32[]{:S(2)}) async-start(), calls=%async_computation.1 | async-start | bytes 2949120 | tf_op jit(solution)/shard_map/psum | solution.py:154
  277.9 2.0 copy-start.37
  279.9 2.3 copy-start.13
  279.9 3.1 copy-start.9
  279.9 3.1 copy-start.18
  279.9 4.0 copy-start.21
  279.9 4.9 copy-start.35
  279.9 4.9 copy-start.43
  281.9 85.5 %copy-start.11 = (bf16[64,18,34]{0,2,1:T(8,128)(2,1)S(1)}, bf16[64,18,34]{0,2,1:T(8,128)(2,1)}, u32[]{:S(2)}) copy-start(bf16[64,18,34]{0,2,1:T(8,128)(2,1)} %copy-done.10) | copy-start | bytes 235012
  281.9 85.6 %copy-start.1 = (bf16[64,2,2,20,36]{4,2,1,0,3:T(2,128)(2,1)S(1)}, bf16[64,2,2,20,36]{4,2,1,0,3:T(2,128)(2,1)}, u32[]{:S(2)}) copy-start(bf16[64,2,2,20,36]{4,2,1,0,3:T(2,128)(2,1)} %copy.202) | copy-start | bytes 1105924
  367.4 0.9 copy-start.38
  367.4 0.9 copy-start.40
  367.4 0.9 copy-start.46
Sparse Core Ops, SparseCore 0:
  276.8 90.5 all-reduce.8
  370.1 125.0 all-reduce.6
